TPU v7x, 32 devices: a whole 2x2x4 slice. The times are simulated.
32 devices in a mesh: expert: 8 (over y, x, core), dp: 4 (over z).
Axes of the slice: x: 2, y: 2, z: 4, core: 2. Of those that a mesh axis runs over, the one named last changes fastest.
Arguments:
- tokens: bfloat16 [512, 2048], P(('expert', 'dp')), may hold values from -6 to 6
- out_grad: bfloat16 [512, 2048], P(('expert', 'dp')), may hold values from -6 to 6
- routes: int32 [512, 8], P(('expert', 'dp')), may hold values from 0 to 15, all different within a row; in each aligned block of 16 rows (0 to 15, 16 to 31, ...) at most 16 rows name the same one
- route_gates: float32 [512, 8], P(('expert', 'dp')), may hold values from 0.05 to 0.5
- w_gate: bfloat16 [16, 2048, 384], P('expert'), may hold values from -0.125 to 0.125
- w_up: bfloat16 [16, 2048, 384], P('expert'), may hold values from -0.125 to 0.125
- w_down: bfloat16 [16, 384, 2048], P('expert'), may hold values from -0.3125 to 0.3125
Outputs:
- token_grad: bfloat16 [512, 2048], P(('expert', 'dp'))
- down_grad: float32 [384, 16, 2048], P('dp', 'expert')
Inputs may be any that keep to these rules, and one draw needn't show every extreme that they name: `routes`: each row names 8 different experts. Among the 16 tokens of one device no expert is named more than 16 times, a bound that some block reaches.
All inputs are finite; a program needn't handle non-finite values.
Results may differ from a plain program's by a relative error of at most 0.014.
Values may be sent and summed in bfloat16 or wider, within the bound.
A program may use at most 64 MiB of HBM per device.

v0:
```python
import functools

import jax
import jax.numpy as jnp
from jax import lax
from jax.experimental import pallas as pl
from jax.experimental.pallas import tpu as pltpu
from jax.sharding import PartitionSpec as P

VMEM_BUDGET = 44 << 20
STEPS = 2
ALONG = 1
LAG = 1
NAMES = ("r", "g", "x0", "x1")
NT = (((1,), (1,)), ((), ()))


def gate_up(arrived, w_gate, w_up):
    gate_pre = jnp.einsum("erd,edf->erf", arrived, w_gate, preferred_element_type=jnp.float32)
    up_pre = jnp.einsum("erd,edf->erf", arrived, w_up, preferred_element_type=jnp.float32)
    return (gate_pre, up_pre)


def collective_shards(tokens, out_grad, routes, route_gates, w_gate, w_up, w_down):
    tok_count, model_width = tokens.shape
    top_count = routes.shape[1]
    local_experts = w_gate.shape[0]
    groups = lax.axis_size("expert")
    experts = local_experts * groups
    slot_count = 2 * tok_count * top_count // experts
    flat_routes = routes.reshape(-1)
    onehot = (flat_routes[:, None] == jnp.arange(experts, dtype=jnp.int32)[None, :]).astype(
        jnp.int32
    )
    slot_rank = jnp.sum(onehot * (jnp.cumsum(onehot, axis=0) - onehot), axis=1)
    slot_index = flat_routes * slot_count + slot_rank
    placement = slot_index[None, :] == jnp.arange(experts * slot_count, dtype=jnp.int32)[:, None]
    route_place = placement.astype(jnp.bfloat16)
    token_place = jnp.sum(
        placement.reshape(experts * slot_count, tok_count, top_count).astype(jnp.float32), axis=2
    ).astype(jnp.bfloat16)
    send_inputs = (
        jnp.dot(token_place, tokens, preferred_element_type=jnp.float32)
        .astype(jnp.bfloat16)
        .reshape(experts, slot_count, model_width)
    )
    scaled = (
        (route_gates[:, :, None] * out_grad[:, None, :].astype(jnp.float32))
        .astype(jnp.bfloat16)
        .reshape(tok_count * top_count, model_width)
    )
    send_grads = (
        jnp.dot(route_place, scaled, preferred_element_type=jnp.float32)
        .astype(jnp.bfloat16)
        .reshape(experts, slot_count, model_width)
    )
    arrived, arrived_grad = (
        lax.all_to_all(send_inputs, "expert", split_axis=0, concat_axis=1, tiled=True),
        lax.all_to_all(send_grads, "expert", split_axis=0, concat_axis=1, tiled=True),
    )
    gate_pre, up_pre = gate_up(arrived, w_gate, w_up)
    sigmoid_gate = jax.nn.sigmoid(gate_pre)
    silu_gate = gate_pre * sigmoid_gate
    hidden = (silu_gate * up_pre).astype(jnp.bfloat16)
    hidden_grad = jnp.einsum(
        "erd,efd->erf", arrived_grad, w_down, preferred_element_type=jnp.float32
    )
    gate_grad = (
        hidden_grad * up_pre * (sigmoid_gate + gate_pre * sigmoid_gate * (1.0 - sigmoid_gate))
    ).astype(jnp.bfloat16)
    up_grad = (hidden_grad * silu_gate).astype(jnp.bfloat16)
    row_grads = (
        jnp.einsum("erf,edf->erd", gate_grad, w_gate, preferred_element_type=jnp.float32)
        + jnp.einsum("erf,edf->erd", up_grad, w_up, preferred_element_type=jnp.float32)
    ).astype(jnp.bfloat16)
    returned = lax.all_to_all(row_grads, "expert", split_axis=1, concat_axis=0, tiled=True)
    token_grad = lax.dot_general(
        token_place,
        returned.reshape(experts * slot_count, model_width),
        (((0,), (0,)), ((), ())),
        preferred_element_type=jnp.float32,
    ).astype(jnp.bfloat16)
    hidden_units = hidden.shape[2]
    share_rows = hidden_units // lax.axis_size("dp")
    partial_grad = jnp.einsum(
        "erf,erd->fed", hidden, arrived_grad, preferred_element_type=jnp.float32
    ).astype(jnp.bfloat16)
    total_grad = lax.psum(partial_grad, "dp").astype(jnp.float32)
    first_row = lax.axis_index("dp") * share_rows
    down_grad = lax.dynamic_slice_in_dim(total_grad, first_row, share_rows, 0)
    return (token_grad, down_grad)


def flip(index, bits):
    out, step = index, 1
    while step <= bits:
        if bits & step:
            out = out + step * (1 - 2 * ((index // step) % 2))
        step *= 2
    return out


def copy_keys(chips, planes, local_experts, parts):
    keys = []
    for name in NAMES:
        keys += [(name, d) for d in range(1, chips)] + [(name + "c", d) for d in range(chips)]
    keys += [("z", k) for k in range(1, planes)]
    keys += [("d", k, d) for k in range(planes) for d in range(1, chips)]
    keys += [("dc", k, d) for k in range(planes) for d in range(chips)]
    keys += [("h", k, e) for k in range(1, planes) for e in range(local_experts)]
    keys += [("p", j) for j in range(parts)]
    keys += [("t", j, d) for j in range(parts) for d in range(1, chips)]
    return {key: i for i, key in enumerate(keys)}


def fused_kernel(
    chips, planes, parts, tok, dy, rt, gt, wg, wu, wd, every, hid_in, own_sum, ret_in,
    xb, db, rb, gb, wgv, wuv, wdv, gates, ups, grads, hid_out, grads_g, grads_u,
    keep, pair_out, pair_in, ret_out, lsem, ssem, rsem,
):
    local_experts, model_width, hidden_units = wg.shape
    rows = tok.shape[0]
    count = 2 * chips * rows
    share = hidden_units // planes
    width = model_width // parts
    me, plane = lax.axis_index("expert"), lax.axis_index("dp")
    chip, core = me // 2, me % 2
    partner = {"expert": chip * 2 + 1 - core, "dp": plane}
    across = [{"expert": flip(chip, d) * 2 + core, "dp": plane} for d in range(chips)]
    above = [{"expert": me, "dp": flip(plane, k)} for k in range(planes)]
    keys = copy_keys(chips, planes, local_experts, parts)

    local = []

    def load(src, dst):
        c = pltpu.make_async_copy(src, dst, lsem.at[len(local)])
        c.start()
        local.append(c)
        return c

    own = [load(tok, xb.at[0]), load(rt, rb.at[0]), load(gt, gb.at[0]), load(dy, db.at[0])]
    gate_up_loads = [(load(wg.at[e], wgv.at[e]), load(wu.at[e], wuv.at[e])) for e in range(local_experts)]
    down_loads = [load(wd.at[e], wdv.at[e]) for e in range(local_experts)]

    def remote(key, src, dst, target):
        i = keys[key]
        return pltpu.make_async_remote_copy(
            src_ref=src, dst_ref=dst, send_sem=ssem.at[i], recv_sem=rsem.at[i],
            device_id=target, device_id_type=pl.DeviceIdType.MESH,
        )

    copies = {}
    half = model_width // 2
    for name in NAMES:
        src, buf = {"r": (rt, rb), "g": (gt, gb)}.get(name, (tok, xb))
        cols = pl.ds(int(name[1]) * half, half) if name[0] == "x" else slice(None)
        src = src.at[:, cols]
        for d in range(chips):
            if d:
                copies[name, d] = remote((name, d), src, buf.at[2 * d, :, cols], across[d])
            copies[name + "c", d] = remote(
                (name + "c", d), buf.at[2 * d, :, cols] if d else src, buf.at[2 * d + 1, :, cols], partner
            )
    for k in range(planes):
        blocks = every.at[k] if k else db
        if k:
            copies["z", k] = remote(("z", k), dy, blocks.at[0], above[k])
        first = blocks.at[0] if k else dy
        for d in range(chips):
            if 0 < k <= ALONG and d == chips - 1:
                copies["d", k, d] = remote(("d", k, d), db.at[2 * d], blocks.at[2 * d], above[k])
            elif d:
                copies["d", k, d] = remote(("d", k, d), first, blocks.at[2 * d], across[d])
            copies["dc", k, d] = remote(
                ("dc", k, d), blocks.at[2 * d] if d else first, blocks.at[2 * d + 1], partner
            )
    for k in range(1, planes):
        first = pl.multiple_of(flip(plane, k) * share, 16)
        for e in range(local_experts):
            copies["h", k, e] = remote(
                ("h", k, e), hid_out.at[e, pl.ds(first, share)], hid_in.at[k, e], above[k]
            )
    for j in range(parts):
        copies["p", j] = remote(("p", j), pair_out.at[j], pair_in.at[j], partner)
        for d in range(1, chips):
            copies["t", j, d] = remote(
                ("t", j, d), ret_out.at[j, d], ret_in.at[d - 1, :, pl.ds(j * width, width)], across[d]
            )

    barrier = pltpu.get_barrier_semaphore()
    targets = [partner] + across[1:] + above[1:]
    for target in targets:
        pl.semaphore_signal(barrier, inc=1, device_id=target, device_id_type=pl.DeviceIdType.MESH)
    pl.semaphore_wait(barrier, len(targets))

    for d in range(chips - 1, 0, -1):
        copies["d", 0, d].start()
    for k in range(planes - 1, 0, -1):
        copies["z", k].start()
    for name in NAMES:
        for d in range(chips - 1, 0, -1):
            copies[name, d].start()
    copies["dc", 0, 0].start()
    for name in NAMES:
        copies[name + "c", 0].start()
    for d in range(chips - 1, 0, -1):
        copies["d", 0, d].wait_recv()
        copies["dc", 0, d].start()
        if d == chips - 1:
            for k in range(1, min(planes, ALONG + 1)):
                copies["d", k, d].start()
    for k in range(1, planes):
        copies["z", k].wait_recv()
        for d in range(chips - 1, 0, -1):
            if d < chips - 1 or k > ALONG:
                copies["d", k, d].start()
        copies["dc", k, 0].start()
    for c in own:
        c.wait()
    for d in range(chips):
        copies["dc", 0, d].wait_recv()
    load(db, every.at[0])
    grad_rows = db[...].reshape(count, model_width)
    for e in range(local_experts):
        down_loads[e].wait()
        grads[e] = lax.dot_general(grad_rows, wdv[e], NT, preferred_element_type=jnp.float32)

    for name in NAMES:
        for d in range(chips - 1, 0, -1):
            copies[name, d].wait_recv()
            copies[name + "c", d].start()
    for name in NAMES:
        for d in range(chips):
            copies[name + "c", d].wait_recv()
        if name[0] == "x":
            begin = int(name[1]) * half
            x = xb[:, :, begin : begin + half].reshape(count, half)
            for e in range(local_experts):
                if begin == 0:
                    for c in gate_up_loads[e]:
                        c.wait()
                for pre, weights in ((gates, wgv), (ups, wuv)):
                    term = jnp.dot(
                        x, weights[e, begin : begin + half, :], preferred_element_type=jnp.float32
                    )
                    pre[e] = term if begin == 0 else pre[e] + term

    named, given = rb[...], gb[...]
    diagonal = lax.broadcasted_iota(jnp.int32, (1, rows, rows), 1) == lax.broadcasted_iota(
        jnp.int32, (1, rows, rows), 2
    )
    for e in range(local_experts):
        gain = jnp.sum(
            jnp.where(named == me * local_experts + e, given, 0.0), axis=1, keepdims=True
        )
        gain = jnp.sum(jnp.where(diagonal, gain, 0.0), axis=2, keepdims=True).reshape(count, 1)
        hidden_grad = gain * grads[e]
        gate_pre, up_pre = gates[e], ups[e]
        s = jax.nn.sigmoid(gate_pre)
        silu = gate_pre * s
        ups[e] = silu * up_pre * gain
        grads_g[e] = (hidden_grad * up_pre * (s + gate_pre * s * (1.0 - s))).astype(jnp.bfloat16)
        grads_u[e] = (hidden_grad * silu).astype(jnp.bfloat16)

    for j in range(parts + LAG):
        if j < parts:
            cols = pl.ds(j * width, width)
            total = None
            for e in range(local_experts):
                for rows_grad, weights in ((grads_g, wgv), (grads_u, wuv)):
                    term = lax.dot_general(
                        rows_grad[e], weights[e, cols, :], NT, preferred_element_type=jnp.float32
                    )
                    total = term if total is None else total + term
            total = total.reshape(chips, 2, rows, width)
            pair_out[j] = total[:, 1].astype(jnp.bfloat16)
            copies["p", j].start()
            keep[j] = total[:, 0]
        if j == parts - 1:
            for e in range(local_experts):
                hid_out[e] = ups[e].T.astype(jnp.bfloat16)
            for k in range(1, planes):
                for e in range(local_experts):
                    copies["h", k, e].start()
            first = pl.multiple_of(plane * share, 16)
            for e in range(local_experts):
                load(hid_out.at[e, pl.ds(first, share)], hid_in.at[0, e])
        if j >= LAG:
            i = j - LAG
            copies["p", i].wait_recv()
            total = keep[i] + pair_in[i].astype(jnp.float32)
            for d in range(chips - 1, 0, -1):
                ret_out[i, d] = total[d].astype(jnp.bfloat16)
            for d in range(chips - 1, 0, -1):
                copies["t", i, d].start()
            keep[i, 0] = total[0]
            load(keep.at[i, 0], own_sum.at[:, pl.ds(i * width, width)])

    for k in range(1, planes):
        for d in range(1, chips):
            copies["d", k, d].wait_recv()
            copies["dc", k, d].start()

    for k in range(1, planes):
        for e in range(local_experts):
            copies["h", k, e].wait_recv()
        for d in range(chips):
            copies["dc", k, d].wait_recv()
    for j in range(parts):
        for d in range(1, chips):
            copies["t", j, d].wait_recv()
    for c in local[len(own) + 3 * local_experts :]:
        c.wait()
    for c in copies.values():
        c.wait_send()


def finish_kernel(
    every, hid, own_sum, returned, token_out, down_out,
    every_v, hid_v, own_v, returned_v, token_v, down_v, sems,
):
    planes, local_experts, share, count = hid.shape
    width = every.shape[1] // STEPS
    blocks = width // 128
    started = []

    def copy(src, dst):
        c = pltpu.make_async_copy(src, dst, sems.at[len(started)])
        c.start()
        started.append(c)
        return c

    hid_load = copy(hid, hid_v)
    loads = [
        copy(every.at[:, pl.ds(i * width, width)], every_v.at[:, pl.ds(i * width, width)])
        for i in range(STEPS)
    ]
    last_loads = [copy(own_sum, own_v), copy(returned, returned_v)]
    hid_load.wait()
    pieces = [hid_v[k].reshape(local_experts * share, count) for k in range(planes)]
    pieces = jnp.concatenate(pieces, axis=1)
    stores = []
    for i in range(STEPS):
        loads[i].wait()
        result = jnp.dot(
            pieces, every_v[:, i * width : (i + 1) * width], preferred_element_type=jnp.float32
        )
        lines = down_v.at[i].reshape(share * blocks * local_experts, 128)
        for e in range(local_experts):
            for b in range(blocks):
                lines[pl.ds(b * local_experts + e, share, stride=blocks * local_experts), :] = (
                    result[e * share : (e + 1) * share, b * 128 : (b + 1) * 128]
                )
        stores.append(
            copy(down_v.at[i], down_out.at[:, pl.ds(i * blocks * local_experts, blocks * local_experts)])
        )
        if i == 0:
            for c in last_loads:
                c.wait()
            total = own_v[...]
            for d in range(returned.shape[0]):
                total = total + returned_v[d].astype(jnp.float32)
            token_v[...] = total.astype(jnp.bfloat16)
            stores.append(copy(token_v, token_out))
    for c in stores:
        c.wait()


def fused_shapes(chips, planes, parts, rows, top, local_experts, model_width, hidden_units):
    bf16, f32 = jnp.bfloat16, jnp.float32
    count, width = 2 * chips * rows, model_width // parts
    return [
        ((2 * chips, rows, model_width), bf16),
        ((2 * chips, rows, model_width), bf16),
        ((2 * chips, top, rows), jnp.int32),
        ((2 * chips, top, rows), f32),
        ((local_experts, model_width, hidden_units), bf16),
        ((local_experts, model_width, hidden_units), bf16),
        ((local_experts, hidden_units, model_width), bf16),
        ((local_experts, count, hidden_units), f32),
        ((local_experts, count, hidden_units), f32),
        ((local_experts, count, hidden_units), f32),
        ((local_experts, hidden_units, count), bf16),
        ((local_experts, count, hidden_units), bf16),
        ((local_experts, count, hidden_units), bf16),
        ((parts, chips, rows, width), f32),
        ((parts, chips, rows, width), bf16),
        ((parts, chips, rows, width), bf16),
        ((parts, chips, rows, width), bf16),
    ]


def buffer_bytes(shapes):
    total = 0
    for dims, kind in shapes:
        size = jnp.dtype(kind).itemsize
        for dim in dims[:-1]:
            size *= dim
        total += size * (-(-dims[-1] // 128) * 128)
    return total


def plan(tokens, routes, w_gate):
    groups, planes = lax.axis_size("expert"), lax.axis_size("dp")
    chips, parts = groups // 2, 2
    rows, model_width = tokens.shape
    local_experts, _, hidden_units = w_gate.shape
    if groups % 2 or chips & (chips - 1) or planes & (planes - 1):
        return None
    if rows % 16 or hidden_units % (16 * planes) or (groups * rows) % 128 or model_width % (512 * STEPS):
        return None
    shapes = fused_shapes(
        chips, planes, parts, rows, routes.shape[1], local_experts, model_width, hidden_units
    )
    if buffer_bytes(shapes) > VMEM_BUDGET:
        return None
    return chips, planes, parts, shapes


def shards(tokens, out_grad, routes, route_gates, w_gate, w_up, w_down):
    planned = plan(tokens, routes, w_gate)
    if planned is None:
        return collective_shards(tokens, out_grad, routes, route_gates, w_gate, w_up, w_down)
    chips, planes, parts, shapes = planned
    rows, model_width = tokens.shape
    local_experts, _, hidden_units = w_gate.shape
    share = hidden_units // planes
    amount = len(copy_keys(chips, planes, local_experts, parts))
    count = 2 * chips * rows
    anywhere = pl.BlockSpec(memory_space=pl.ANY)
    every, hid, own_sum, returned = pl.pallas_call(
        functools.partial(fused_kernel, chips, planes, parts),
        out_shape=(
            jax.ShapeDtypeStruct((planes, 2 * chips, rows, model_width), jnp.bfloat16),
            jax.ShapeDtypeStruct((planes, local_experts, share, count), jnp.bfloat16),
            jax.ShapeDtypeStruct((rows, model_width), jnp.float32),
            jax.ShapeDtypeStruct((chips - 1, rows, model_width), jnp.bfloat16),
        ),
        in_specs=[anywhere] * 7,
        out_specs=(anywhere,) * 4,
        scratch_shapes=[pltpu.VMEM(dims, kind) for dims, kind in shapes]
        + [
            pltpu.SemaphoreType.DMA((5 + 4 * local_experts + parts,)),
            pltpu.SemaphoreType.DMA((amount,)),
            pltpu.SemaphoreType.DMA((amount,)),
        ],
        compiler_params=pltpu.CompilerParams(
            collective_id=0, has_side_effects=True, vmem_limit_bytes=60 << 20
        ),
        name="expert_backward",
    )(tokens, out_grad, routes.T, route_gates.T, w_gate, w_up, w_down)
    width = model_width // STEPS
    lines = width // 128 * local_experts
    token_grad, down_grad = pl.pallas_call(
        finish_kernel,
        out_shape=(
            jax.ShapeDtypeStruct((rows, model_width), jnp.bfloat16),
            jax.ShapeDtypeStruct((share, model_width // 128 * local_experts, 128), jnp.float32),
        ),
        in_specs=[anywhere] * 4,
        out_specs=(anywhere,) * 2,
        scratch_shapes=[
            pltpu.VMEM((planes * count, model_width), jnp.bfloat16),
            pltpu.VMEM(hid.shape, jnp.bfloat16),
            pltpu.VMEM((rows, model_width), jnp.float32),
            pltpu.VMEM((chips - 1, rows, model_width), jnp.bfloat16),
            pltpu.VMEM((rows, model_width), jnp.bfloat16),
            pltpu.VMEM((STEPS, share, lines, 128), jnp.float32),
            pltpu.SemaphoreType.DMA((4 + 2 * STEPS,)),
        ],
        compiler_params=pltpu.CompilerParams(vmem_limit_bytes=60 << 20),
        name="expert_finish",
    )(every.reshape(planes * count, model_width), hid, own_sum, returned)
    down_grad = down_grad.reshape(share, model_width // 128, local_experts, 128)
    return (token_grad, down_grad.transpose(0, 2, 1, 3).reshape(share, local_experts, model_width))


def solution(mesh):
    placed = (
        P(("expert", "dp"), None),
        P(("expert", "dp"), None),
        P(("expert", "dp"), None),
        P(("expert", "dp"), None),
        P("expert", None, None),
        P("expert", None, None),
        P("expert", None, None),
    )
    return jax.shard_map(
        shards,
        mesh=mesh,
        in_specs=placed,
        out_specs=(P(("expert", "dp"), None), P("dp", "expert", None)),
        check_vma=False,
    )
```

profile of v0, /device:TPU:0, one launch (start us, length us, event | category | flops | bytes accessed | tf_op | source)
XLA Modules:
  0.0 30.1 jit_solution(7050332234248913959)
XLA Ops:
  0.6 26.2 %expert_backward.1 = (bf16[4,8,16,2048]{3,2,1,0:T(8,128)(2,1)}, bf16[4,2,96,128]{3,2,1,0:T(8,128)(2,1)}, f32[16,2048]{1,0:T(8,128)}, bf16[3,16,2048]{2,1,0:T(8,128)(2,1)}) custom-call(bf16[16,2048]{1,0:T(8,128)(2,1)} %tok.1, bf16[16,2048]{1,0:T(8,128)(2,1)} %dy.1, s32[8,16]{1,0:T(8,128)} %bitcast.9, f32[8,16]{1,0:T(8,128)} %bitcast.10, ...), custom_call_target="tpu_custom_call" | custom-call | tf_op jit(solution)/shard_map/expert_backward/pallas_call | solution.py:431
  26.8 3.3 %expert_finish.1 = (bf16[16,2048]{1,0:T(8,128)(2,1)}, f32[96,32,128]{2,1,0:T(8,128)}) custom-call(bf16[512,2048]{1,0:T(8,128)(2,1)} %bitcast.8, bf16[4,2,96,128]{3,2,1,0:T(8,128)(2,1)} %get-tuple-element.9.hid, f32[16,2048]{1,0:T(8,128)} %get-tuple-element.10.own_sum, bf16[3,16,2048]{2,1,0:T(8,128)(2,1)} %get-tuple-element.11.returned), custom_call_target="tpu_custom_call" | custom-call | tf_op jit(solution)/shard_map/expert_finish/pallas_call | solution.py:454
where the time goes:
time: 30.2 us; the launch traced here: 30.1 us
  Pallas kernels  29.5 us (98%)
  between operations  0.64 us (2%)
    pallas_call x1, Pallas kernels, shards(): pl.pallas_call(functools.partial(fused_kernel, chips, planes, parts), out...  26.2 us
    pallas_call x1, Pallas kernels, shards(): pl.pallas_call(finish_kernel, out_shape=(jax.ShapeDtypeStruct((rows, mode...  3.26 us

commit v1 on v0

v1 whole, which is shorter than its diff:
```python
import functools

import jax
import jax.numpy as jnp
from jax import lax
from jax.experimental import pallas as pl
from jax.experimental.pallas import tpu as pltpu
from jax.sharding import PartitionSpec as P

VMEM_BUDGET = 56 << 20
VMEM_PASSED = 4 << 20
STEPS = 2
PARTS = 4
HALVES = 2
ALONG = ((3, 0), (3, 1))
MESH = pl.DeviceIdType.MESH
NT = (((1,), (1,)), ((), ()))


def gate_up(arrived, w_gate, w_up):
    gate_pre = jnp.einsum("erd,edf->erf", arrived, w_gate, preferred_element_type=jnp.float32)
    up_pre = jnp.einsum("erd,edf->erf", arrived, w_up, preferred_element_type=jnp.float32)
    return (gate_pre, up_pre)


def collective_shards(tokens, out_grad, routes, route_gates, w_gate, w_up, w_down):
    tok_count, model_width = tokens.shape
    top_count = routes.shape[1]
    local_experts = w_gate.shape[0]
    groups = lax.axis_size("expert")
    experts = local_experts * groups
    slot_count = 2 * tok_count * top_count // experts
    flat_routes = routes.reshape(-1)
    onehot = (flat_routes[:, None] == jnp.arange(experts, dtype=jnp.int32)[None, :]).astype(
        jnp.int32
    )
    slot_rank = jnp.sum(onehot * (jnp.cumsum(onehot, axis=0) - onehot), axis=1)
    slot_index = flat_routes * slot_count + slot_rank
    placement = slot_index[None, :] == jnp.arange(experts * slot_count, dtype=jnp.int32)[:, None]
    route_place = placement.astype(jnp.bfloat16)
    token_place = jnp.sum(
        placement.reshape(experts * slot_count, tok_count, top_count).astype(jnp.float32), axis=2
    ).astype(jnp.bfloat16)
    send_inputs = (
        jnp.dot(token_place, tokens, preferred_element_type=jnp.float32)
        .astype(jnp.bfloat16)
        .reshape(experts, slot_count, model_width)
    )
    scaled = (
        (route_gates[:, :, None] * out_grad[:, None, :].astype(jnp.float32))
        .astype(jnp.bfloat16)
        .reshape(tok_count * top_count, model_width)
    )
    send_grads = (
        jnp.dot(route_place, scaled, preferred_element_type=jnp.float32)
        .astype(jnp.bfloat16)
        .reshape(experts, slot_count, model_width)
    )
    arrived, arrived_grad = (
        lax.all_to_all(send_inputs, "expert", split_axis=0, concat_axis=1, tiled=True),
        lax.all_to_all(send_grads, "expert", split_axis=0, concat_axis=1, tiled=True),
    )
    gate_pre, up_pre = gate_up(arrived, w_gate, w_up)
    sigmoid_gate = jax.nn.sigmoid(gate_pre)
    silu_gate = gate_pre * sigmoid_gate
    hidden = (silu_gate * up_pre).astype(jnp.bfloat16)
    hidden_grad = jnp.einsum(
        "erd,efd->erf", arrived_grad, w_down, preferred_element_type=jnp.float32
    )
    gate_grad = (
        hidden_grad * up_pre * (sigmoid_gate + gate_pre * sigmoid_gate * (1.0 - sigmoid_gate))
    ).astype(jnp.bfloat16)
    up_grad = (hidden_grad * silu_gate).astype(jnp.bfloat16)
    row_grads = (
        jnp.einsum("erf,edf->erd", gate_grad, w_gate, preferred_element_type=jnp.float32)
        + jnp.einsum("erf,edf->erd", up_grad, w_up, preferred_element_type=jnp.float32)
    ).astype(jnp.bfloat16)
    returned = lax.all_to_all(row_grads, "expert", split_axis=1, concat_axis=0, tiled=True)
    token_grad = lax.dot_general(
        token_place,
        returned.reshape(experts * slot_count, model_width),
        (((0,), (0,)), ((), ())),
        preferred_element_type=jnp.float32,
    ).astype(jnp.bfloat16)
    hidden_units = hidden.shape[2]
    share_rows = hidden_units // lax.axis_size("dp")
    partial_grad = jnp.einsum(
        "erf,erd->fed", hidden, arrived_grad, preferred_element_type=jnp.float32
    ).astype(jnp.bfloat16)
    total_grad = lax.psum(partial_grad, "dp").astype(jnp.float32)
    first_row = lax.axis_index("dp") * share_rows
    down_grad = lax.dynamic_slice_in_dim(total_grad, first_row, share_rows, 0)
    return (token_grad, down_grad)


def flip(index, bits):
    out, step = index, 1
    while step <= bits:
        if bits & step:
            out = out + step * (1 - 2 * ((index // step) % 2))
        step *= 2
    return out


def copy_keys(chips, planes, local_experts):
    keys = [("z", k) for k in range(1, planes)] + [("m", i) for i in range(2)]
    for name in ("r", "g"):
        keys += [(name, d) for d in range(1, chips)] + [(name + "c", d) for d in range(chips)]
    keys += [("x", d, h) for d in range(1, chips) for h in range(HALVES)]
    keys += [("xc", d, h) for d in range(chips) for h in range(HALVES)]
    keys += [("d", k, d, h) for k in range(planes) for d in range(1, chips) for h in range(HALVES)]
    keys += [("dc", 0, d, h) for d in range(chips) for h in range(HALVES)]
    keys += [("dc", k, d) for k in range(1, planes) for d in range(chips)]
    keys += [("h", k, e) for k in range(1, planes) for e in range(local_experts)]
    keys += [("p", j) for j in range(PARTS)]
    keys += [("t", j, d) for j in range(PARTS) for d in range(1, chips)]
    return {key: i for i, key in enumerate(keys)}


def fused_kernel(
    chips, planes, tok, dy, rt, gt, wg, wu, wd, every, hid_in, own_sum, ret_in,
    xb, rb, gb, wide, wdv, pre, grads, hid_f, hid_out, both,
    keep, pair_out, pair_in, ret_out, lsem, ssem, rsem, known,
):
    local_experts, model_width, hidden_units = wg.shape
    rows = tok.shape[0]
    count = 2 * chips * rows
    share = hidden_units // planes
    width = model_width // PARTS
    half = model_width // HALVES
    me, plane = lax.axis_index("expert"), lax.axis_index("dp")
    chip, core = me // 2, me % 2
    inner = (plane % 2) != (plane // 2)
    partner = {"expert": chip * 2 + 1 - core, "dp": plane}
    across = [{"expert": flip(chip, d) * 2 + core, "dp": plane} for d in range(chips)]
    above = [{"expert": me, "dp": flip(plane, k)} for k in range(planes)]
    keys = copy_keys(chips, planes, local_experts)

    local = []

    def load(src, dst):
        c = pltpu.make_async_copy(src, dst, lsem.at[len(local)])
        c.start()
        local.append(c)
        return c

    own = [load(tok, xb.at[0]), load(rt, rb.at[0]), load(gt, gb.at[0]), load(dy, every.at[0, 0])]
    down_loads = [
        load(wd.at[e], wdv.at[pl.ds(e * hidden_units, hidden_units)]) for e in range(local_experts)
    ]
    gate_up_loads = []
    for e in range(local_experts):
        for i, w in enumerate((wg, wu)):
            gate_up_loads.append(
                load(w.at[e], wide.at[:, pl.ds((2 * e + i) * hidden_units, hidden_units)])
            )

    def remote(key, src, dst, target, arrives=None):
        return pltpu.make_async_remote_copy(
            src_ref=src, dst_ref=dst, send_sem=ssem.at[keys[key]],
            recv_sem=rsem.at[keys[arrives or key]], device_id=target, device_id_type=MESH,
        )

    def cols(h):
        return pl.ds(h * half, half)

    copies, inner_copies = {}, {}
    for name, src, buf in (("r", rt, rb), ("g", gt, gb)):
        for d in range(chips):
            if d:
                copies[name, d] = remote((name, d), src, buf.at[2 * d], across[d])
            copies[name + "c", d] = remote(
                (name + "c", d), buf.at[2 * d] if d else src, buf.at[2 * d + 1], partner
            )

    def spread(name, first, buf, lead):
        for h in range(HALVES):
            for d in (1, 2):
                copies[(name,) + lead + (d, h)] = remote(
                    (name,) + lead + (d, h), first.at[:, cols(h)], buf.at[2 * d, :, cols(h)], across[d]
                )
            via, to = (1, 2) if h == 0 else (2, 1)
            copies[(name,) + lead + (3, h)] = remote(
                (name,) + lead + (3, h), buf.at[2 * via, :, cols(h)], buf.at[6, :, cols(h)], across[to]
            )

    spread("x", tok, xb, ())
    for d in range(chips):
        for h in range(HALVES):
            for key, first, buf in ((("xc",), tok, xb), (("dc", 0), dy, every.at[0])):
                copies[key + (d, h)] = remote(
                    key + (d, h),
                    buf.at[2 * d, :, cols(h)] if d else first.at[:, cols(h)],
                    buf.at[2 * d + 1, :, cols(h)],
                    partner,
                )
    for k in range(planes):
        spread("d", every.at[k, 0] if k else dy, every.at[k], (k,))
        if k:
            for d in range(chips):
                copies["dc", k, d] = remote(
                    ("dc", k, d), every.at[k, 2 * d], every.at[k, 2 * d + 1], partner
                )
            copies["z", k] = remote(("z", k), dy, every.at[k, 0], above[k])
    for d, h in ALONG:
        copies["d", 1, d, h] = remote(
            ("d", 1, d, h), every.at[0, 2 * d, :, cols(h)], every.at[1, 2 * d, :, cols(h)], above[1]
        )
    for k in range(1, planes):
        first = pl.multiple_of(flip(plane, k) * share, 16)
        for e in range(local_experts):
            copies["h", k, e] = remote(
                ("h", k, e), hid_out.at[e, pl.ds(first, share)], hid_in.at[k, e], above[k]
            )
    for j in range(PARTS):
        copies["p", j] = remote(("p", j), pair_out.at[j], pair_in.at[j], partner)
        for d in range(1, chips):
            copies["t", j, d] = remote(
                ("t", j, d), ret_out.at[j, d], ret_in.at[d - 1, :, pl.ds(j * width, width)], across[d]
            )

    def start(*key):
        copies[key].start()

    def arrive(*key):
        copies[key].wait_recv()

    def relay(name, lead=()):
        for d, h in ((1, 0), (2, 1)):
            arrive(name, *lead, d, h)
            if name == "x" or lead[0] != 1 or (3, h) not in ALONG:
                start(name, *lead, 3, h)
            if name == "x" or lead[0] == 0:
                start(name + "c", *lead, d, h)

    def rest(name, lead=()):
        for d, h in ((1, 1), (2, 0)):
            arrive(name, *lead, d, h)
            if name == "x" or lead[0] == 0:
                start(name + "c", *lead, d, h)
            else:
                start("dc", *lead, d)

    def send_plane(k):
        for h in range(HALVES):
            for d in (1, 2):
                piece = (d, h if d == 1 else 1 - h)
                if k != 1 or piece not in ALONG:
                    start("d", k, *piece)

    barrier = pltpu.get_barrier_semaphore()
    for target in [partner] + across[1:3] + [above[1]]:
        pl.semaphore_signal(barrier, inc=1, device_id=target, device_id_type=MESH)

    @pl.when(inner)
    def _():
        pl.semaphore_signal(barrier, inc=1, device_id=above[3], device_id_type=MESH)

    pl.semaphore_wait(barrier, 4 + inner.astype(jnp.int32))

    @pl.when(inner)
    def _():
        pl.semaphore_signal(known, inc=1, device_id=above[3], device_id_type=MESH)
        copies["z", 3].start()

    send_plane(0)
    start("z", 1)
    for h in range(HALVES):
        start("dc", 0, 0, h)
    for name in ("r", "g"):
        for d in (1, 2):
            start(name, d)
        start(name + "c", 0)
    for h in range(HALVES):
        start("x", 1, h)
        start("x", 2, 1 - h)
        start("xc", 0, h)

    @pl.when(inner)
    def _():
        pl.semaphore_wait(known, 1)
        pl.semaphore_signal(known, inc=1, device_id=above[1], device_id_type=MESH)
        copies["z", 2].start()

    relay("d", (0,))
    rest("d", (0,))
    for name in ("r", "g"):
        start(name, 3)

    @pl.when(jnp.logical_not(inner))
    def _():
        pl.semaphore_wait(known, 1)
        copies["z", 3].start()
        copies["z", 2].start()

    relay("x")
    rest("x")
    for name in ("r", "g"):
        for d in (1, 2):
            arrive(name, d)
            start(name + "c", d)
    arrive("z", 1)
    send_plane(1)
    start("dc", 1, 0)
    for h in range(HALVES):
        arrive("d", 0, 3, h)
        start("dc", 0, 3, h)
    for d, h in ALONG:
        start("d", 1, d, h)
    for h in range(HALVES):
        arrive("x", 3, h)
        start("xc", 3, h)
    for name in ("r", "g"):
        arrive(name, 3)
        start(name + "c", 3)

    for c in own:
        c.wait()
    for c in down_loads:
        c.wait()
    for h in range(HALVES):
        for d in range(chips):
            arrive("dc", 0, d, h)
        begin = h * half
        term = lax.dot_general(
            wdv[:, begin : begin + half],
            every[0, :, :, begin : begin + half].reshape(count, half),
            NT,
            preferred_element_type=jnp.float32,
        ).T
        grads[...] = grads[...] + term if h else term
    arrive("z", 2)
    send_plane(2)
    start("dc", 2, 0)
    for c in gate_up_loads:
        c.wait()
    for h in range(HALVES):
        for d in range(chips):
            arrive("xc", d, h)
        begin = h * half
        term = jnp.dot(
            xb[:, :, begin : begin + half].reshape(count, half),
            wide[begin : begin + half, :],
            preferred_element_type=jnp.float32,
        )
        pre[...] = pre[...] + term if h else term
        if h == 0:
            relay("d", (1,))
    arrive("z", 3)
    send_plane(3)
    start("dc", 3, 0)
    for name in ("r", "g"):
        for d in range(chips):
            arrive(name + "c", d)

    named, given = rb[...], gb[...]
    diagonal = lax.broadcasted_iota(jnp.int32, (1, rows, rows), 1) == lax.broadcasted_iota(
        jnp.int32, (1, rows, rows), 2
    )
    for e in range(local_experts):
        gain = jnp.sum(
            jnp.where(named == me * local_experts + e, given, 0.0), axis=1, keepdims=True
        )
        gain = jnp.sum(jnp.where(diagonal, gain, 0.0), axis=2, keepdims=True).reshape(count, 1)
        a, b, c = ((2 * e + i) * hidden_units for i in range(3))
        hidden_grad = gain * grads[:, e * hidden_units : (e + 1) * hidden_units]
        gate_pre, up_pre = pre[:, a:b], pre[:, b:c]
        s = jax.nn.sigmoid(gate_pre)
        silu = gate_pre * s
        hid_f[e] = silu * up_pre * gain
        both[:, a:b] = (hidden_grad * up_pre * (s + gate_pre * s * (1.0 - s))).astype(jnp.bfloat16)
        both[:, b:c] = (hidden_grad * silu).astype(jnp.bfloat16)

    hid_loads = []
    for j in range(PARTS + 1):
        if j < PARTS:
            total = lax.dot_general(
                wide[j * width : (j + 1) * width, :], both[...], NT, preferred_element_type=jnp.float32
            ).T.reshape(chips, 2, rows, width)
            pair_out[j] = total[:, 1].astype(jnp.bfloat16)
            start("p", j)
            keep[j] = total[:, 0]
        if j == 0:
            rest("d", (1,))
        if j == 1:
            for e in range(local_experts):
                hid_out[e] = hid_f[e].T.astype(jnp.bfloat16)
            for k in range(1, planes):
                for e in range(local_experts):
                    start("h", k, e)
            first = pl.multiple_of(plane * share, 16)
            for e in range(local_experts):
                hid_loads.append(load(hid_out.at[e, pl.ds(first, share)], hid_in.at[0, e]))
            relay("d", (2,))
        if j == 2:
            rest("d", (2,))
        if j == 3:
            relay("d", (3,))
        if j:
            i = j - 1
            arrive("p", i)
            total = keep[i] + pair_in[i].astype(jnp.float32)
            for d in range(chips - 1, 0, -1):
                ret_out[i, d] = total[d].astype(jnp.bfloat16)
            for d in range(chips - 1, 0, -1):
                start("t", i, d)
            own_sum[:, i * width : (i + 1) * width] = total[0]

    rest("d", (3,))
    for k in range(1, planes):
        for h in range(HALVES):
            arrive("d", k, 3, h)
        start("dc", k, 3)
    for k in range(1, planes):
        for e in range(local_experts):
            arrive("h", k, e)
        for d in range(chips):
            arrive("dc", k, d)
    for j in range(PARTS):
        for d in range(1, chips):
            arrive("t", j, d)
    for c in hid_loads:
        c.wait()
    for c in copies.values():
        c.wait_send()


def finish_kernel(
    every, hid, own_sum, returned, token_out, down_out, token_v, down_v, sems
):
    planes, local_experts, share, count = hid.shape
    model_width = every.shape[3]
    width = model_width // STEPS
    blocks = width // 128
    stores = []

    def store(src, dst):
        c = pltpu.make_async_copy(src, dst, sems.at[len(stores)])
        c.start()
        stores.append(c)

    pieces = [hid[k].reshape(local_experts * share, count) for k in range(planes)]
    pieces = jnp.concatenate(pieces, axis=1)
    for i in range(STEPS):
        result = jnp.dot(
            pieces,
            every[:, :, :, i * width : (i + 1) * width].reshape(planes * count, width),
            preferred_element_type=jnp.float32,
        )
        lines = down_v.at[i].reshape(share * blocks * local_experts, 128)
        for e in range(local_experts):
            for b in range(blocks):
                lines[pl.ds(b * local_experts + e, share, stride=blocks * local_experts), :] = (
                    result[e * share : (e + 1) * share, b * 128 : (b + 1) * 128]
                )
        store(
            down_v.at[i], down_out.at[:, pl.ds(i * blocks * local_experts, blocks * local_experts)]
        )
        if i == 0:
            total = own_sum[...]
            for d in range(returned.shape[0]):
                total = total + returned[d].astype(jnp.float32)
            token_v[...] = total.astype(jnp.bfloat16)
            store(token_v, token_out)
    for c in stores:
        c.wait()


def fused_shapes(chips, planes, rows, top, local_experts, model_width, hidden_units):
    bf16, f32 = jnp.bfloat16, jnp.float32
    count, width = 2 * chips * rows, model_width // PARTS
    return [
        ((2 * chips, rows, model_width), bf16),
        ((2 * chips, top, rows), jnp.int32),
        ((2 * chips, top, rows), f32),
        ((model_width, 2 * local_experts * hidden_units), bf16),
        ((local_experts * hidden_units, model_width), bf16),
        ((count, 2 * local_experts * hidden_units), f32),
        ((count, local_experts * hidden_units), f32),
        ((local_experts, count, hidden_units), f32),
        ((local_experts, hidden_units, count), bf16),
        ((count, 2 * local_experts * hidden_units), bf16),
        ((PARTS, chips, rows, width), f32),
        ((PARTS, chips, rows, width), bf16),
        ((PARTS, chips, rows, width), bf16),
        ((PARTS, chips, rows, width), bf16),
    ]


def buffer_bytes(shapes):
    total = 0
    for dims, kind in shapes:
        size = jnp.dtype(kind).itemsize
        for dim in dims[:-1]:
            size *= dim
        total += size * (-(-dims[-1] // 128) * 128)
    return total


def plan(tokens, routes, w_gate):
    groups, planes = lax.axis_size("expert"), lax.axis_size("dp")
    chips = groups // 2
    rows, model_width = tokens.shape
    local_experts, _, hidden_units = w_gate.shape
    if groups != 8 or planes != 4:
        return None
    if rows % 16 or hidden_units % 128 or (groups * rows) % 128 or model_width % (128 * PARTS):
        return None
    shapes = fused_shapes(
        chips, planes, rows, routes.shape[1], local_experts, model_width, hidden_units
    )
    passed = planes * groups * rows * model_width * 2
    if buffer_bytes(shapes) > VMEM_BUDGET or passed > VMEM_PASSED:
        return None
    return chips, planes, shapes


def shards(tokens, out_grad, routes, route_gates, w_gate, w_up, w_down):
    planned = plan(tokens, routes, w_gate)
    if planned is None:
        return collective_shards(tokens, out_grad, routes, route_gates, w_gate, w_up, w_down)
    chips, planes, shapes = planned
    rows, model_width = tokens.shape
    local_experts, _, hidden_units = w_gate.shape
    share = hidden_units // planes
    amount = len(copy_keys(chips, planes, local_experts))
    count = 2 * chips * rows
    outside = pl.BlockSpec(memory_space=pltpu.HBM)
    inside = pl.BlockSpec(memory_space=pltpu.VMEM)
    passed = pl.pallas_call(
        functools.partial(fused_kernel, chips, planes),
        out_shape=(
            pltpu.VMEM((planes, 2 * chips, rows, model_width), jnp.bfloat16),
            pltpu.VMEM((planes, local_experts, share, count), jnp.bfloat16),
            pltpu.VMEM((rows, model_width), jnp.float32),
            pltpu.VMEM((chips - 1, rows, model_width), jnp.bfloat16),
        ),
        in_specs=[outside] * 7,
        out_specs=(inside,) * 4,
        scratch_shapes=[pltpu.VMEM(dims, kind) for dims, kind in shapes]
        + [
            pltpu.SemaphoreType.DMA((4 + 5 * local_experts,)),
            pltpu.SemaphoreType.DMA((amount,)),
            pltpu.SemaphoreType.DMA((amount,)),
            pltpu.SemaphoreType.REGULAR,
        ],
        compiler_params=pltpu.CompilerParams(
            collective_id=0, has_side_effects=True, vmem_limit_bytes=VMEM_BUDGET
        ),
        name="expert_backward",
    )(tokens, out_grad, routes.T, route_gates.T, w_gate, w_up, w_down)
    width = model_width // STEPS
    lines = width // 128 * local_experts
    token_grad, down_grad = pl.pallas_call(
        finish_kernel,
        out_shape=(
            jax.ShapeDtypeStruct((rows, model_width), jnp.bfloat16),
            jax.ShapeDtypeStruct((share, model_width // 128 * local_experts, 128), jnp.float32),
        ),
        in_specs=[inside] * 4,
        out_specs=(outside,) * 2,
        scratch_shapes=[
            pltpu.VMEM((rows, model_width), jnp.bfloat16),
            pltpu.VMEM((STEPS, share, lines, 128), jnp.float32),
            pltpu.SemaphoreType.DMA((1 + STEPS,)),
        ],
        compiler_params=pltpu.CompilerParams(vmem_limit_bytes=32 << 20),
        name="expert_finish",
    )(*passed)
    down_grad = down_grad.reshape(share, model_width // 128, local_experts, 128)
    return (token_grad, down_grad.transpose(0, 2, 1, 3).reshape(share, local_experts, model_width))


def solution(mesh):
    placed = (
        P(("expert", "dp"), None),
        P(("expert", "dp"), None),
        P(("expert", "dp"), None),
        P(("expert", "dp"), None),
        P("expert", None, None),
        P("expert", None, None),
        P("expert", None, None),
    )
    return jax.shard_map(
        shards,
        mesh=mesh,
        in_specs=placed,
        out_specs=(P(("expert", "dp"), None), P("dp", "expert", None)),
        check_vma=False,
    )
```

time: 30.2 us -> 29 us (0.960)
  Pallas kernels: 29.5 us -> 28.2 us
    pallas_call x1, Pallas kernels: 3.26 us -> 1.74 us  [shards(): pl.pallas_call(finish_kernel, out_shape=(jax.ShapeDtypeStruct((rows, mode...]
where the time goes in v1:
time: 29 us; the launch traced here: 28.9 us
  Pallas kernels  28.2 us (97%)
  between operations  0.64 us (2%)
    pallas_call x1, Pallas kernels, shards(): pl.pallas_call(functools.partial(fused_kernel, chips, planes), out_shape=...  26.5 us
    pallas_call x1, Pallas kernels, shards(): pl.pallas_call(finish_kernel, out_shape=(jax.ShapeDtypeStruct((rows, mode...  1.74 us

profile of v1, /device:TPU:0, one launch (start us, length us, event | category | flops | bytes accessed | tf_op | source)
XLA Modules:
  0.0 28.9 jit_solution(12931692544154408741)
XLA Ops:
  0.6 26.5 %expert_backward.1 = (bf16[4,8,16,2048]{3,2,1,0:T(8,128)(2,1)S(1)}, bf16[4,2,96,128]{3,2,1,0:T(8,128)(2,1)S(1)}, f32[16,2048]{1,0:T(8,128)S(1)}, bf16[3,16,2048]{2,1,0:T(8,128)(2,1)S(1)}) custom-call(bf16[16,2048]{1,0:T(8,128)(2,1)} %tok.1, bf16[16,2048]{1,0:T(8,128)(2,1)} %dy.1, s32[8,16]{1,0:T(8,128)} %bitcast.7, f32[8,16]{1,0:T(8,128)} %bitcast.8, ...), custom_call_target="tpu_custom_call" | custom-call | tf_op jit(solution)/shard_map/expert_backward/pallas_call | solution.py:530
  27.1 1.7 %expert_finish.1 = (bf16[16,2048]{1,0:T(8,128)(2,1)}, f32[96,32,128]{2,1,0:T(8,128)}) custom-call(bf16[4,8,16,2048]{3,2,1,0:T(8,128)(2,1)S(1)} %get-tuple-element.8.every, bf16[4,2,96,128]{3,2,1,0:T(8,128)(2,1)S(1)} %get-tuple-element.9.hid, f32[16,2048]{1,0:T(8,128)S(1)} %get-tuple-element.10.own_sum, bf16[3,16,2048]{2,1,0:T(8,128)(2,1)S(1)} %get-tuple-element.11.returned), custom_call_target="tpu_custom_call" | custom-call | tf_op jit(solution)/shard_map/expert_finish/pallas_call | solution.py:554

commit v2 on v1

--- a/solution.py
+++ b/solution.py
@@ -1,4 +1,5 @@
 import functools
+import math
 
 import jax
 import jax.numpy as jnp
@@ -102,19 +103,31 @@
     return out
 
 
-def copy_keys(chips, planes, local_experts):
-    keys = [("z", k) for k in range(1, planes)] + [("m", i) for i in range(2)]
-    for name in ("r", "g"):
-        keys += [(name, d) for d in range(1, chips)] + [(name + "c", d) for d in range(chips)]
-    keys += [("x", d, h) for d in range(1, chips) for h in range(HALVES)]
-    keys += [("xc", d, h) for d in range(chips) for h in range(HALVES)]
-    keys += [("d", k, d, h) for k in range(planes) for d in range(1, chips) for h in range(HALVES)]
-    keys += [("dc", 0, d, h) for d in range(chips) for h in range(HALVES)]
-    keys += [("dc", k, d) for k in range(1, planes) for d in range(chips)]
-    keys += [("h", k, e) for k in range(1, planes) for e in range(local_experts)]
-    keys += [("p", j) for j in range(PARTS)]
-    keys += [("t", j, d) for j in range(PARTS) for d in range(1, chips)]
-    return {key: i for i, key in enumerate(keys)}
+def arrival_groups(planes):
+    names = ["r", "g", "rc", "gc", "h", "t"]
+    names += [("z", k) for k in range(1, planes)]
+    for lead in [("x",)] + [("d", k) for k in range(planes)]:
+        names += [lead + (1, 0), lead + (2, 1), lead + ("rest",), lead + (3,)]
+    names += [(name, h) for name in ("xc", "dc") for h in range(HALVES)]
+    names += [("dk", k) for k in range(1, planes)] + [("p", j) for j in range(PARTS)]
+    return {name: i for i, name in enumerate(names)}
+
+
+def group_of(key):
+    name = key[0]
+    if name in ("z", "p"):
+        return key
+    if name in ("r", "g", "rc", "gc", "h", "t"):
+        return name
+    if name in ("xc", "dc"):
+        return (name, key[2])
+    if name == "dk":
+        return key[:2]
+    d, h = key[-2:]
+    lead = key[:-2]
+    if d == 3:
+        return lead + (3,)
+    return lead + ((d, h) if (d, h) in ((1, 0), (2, 1)) else ("rest",))
 
 
 def fused_kernel(
@@ -134,37 +147,39 @@
     partner = {"expert": chip * 2 + 1 - core, "dp": plane}
     across = [{"expert": flip(chip, d) * 2 + core, "dp": plane} for d in range(chips)]
     above = [{"expert": me, "dp": flip(plane, k)} for k in range(planes)]
-    keys = copy_keys(chips, planes, local_experts)
-
-    local = []
-
-    def load(src, dst):
-        c = pltpu.make_async_copy(src, dst, lsem.at[len(local)])
+    groups = arrival_groups(planes)
+
+    def load(src, dst, i):
+        c = pltpu.make_async_copy(src, dst, lsem.at[i])
         c.start()
-        local.append(c)
         return c
 
-    own = [load(tok, xb.at[0]), load(rt, rb.at[0]), load(gt, gb.at[0]), load(dy, every.at[0, 0])]
-    down_loads = [
-        load(wd.at[e], wdv.at[pl.ds(e * hidden_units, hidden_units)]) for e in range(local_experts)
+    own = [
+        load(src, dst, i)
+        for i, (src, dst) in enumerate(
+            ((dy, every.at[0, 0]), (tok, xb.at[0]), (rt, rb.at[0]), (gt, gb.at[0]))
+        )
     ]
-    gate_up_loads = []
-    for e in range(local_experts):
-        for i, w in enumerate((wg, wu)):
-            gate_up_loads.append(
-                load(w.at[e], wide.at[:, pl.ds((2 * e + i) * hidden_units, hidden_units)])
-            )
-
-    def remote(key, src, dst, target, arrives=None):
+
+    def load_weights():
+        load(wd, wdv, 4)
+        for e in range(local_experts):
+            for i, w in enumerate((wg, wu)):
+                load(w.at[e], wide.at[:, pl.ds((2 * e + i) * hidden_units, hidden_units)], 5)
+
+    def remote(key, src, dst, target):
         return pltpu.make_async_remote_copy(
-            src_ref=src, dst_ref=dst, send_sem=ssem.at[keys[key]],
-            recv_sem=rsem.at[keys[arrives or key]], device_id=target, device_id_type=MESH,
+            src_ref=src, dst_ref=dst, send_sem=ssem.at[{"r": 1, "g": 2}.get(key[0][0], 0)],
+            recv_sem=rsem.at[groups[group_of(key)]], device_id=target, device_id_type=MESH,
         )
+
+    def whole(ref, sem):
+        pltpu.make_async_copy(ref, ref, sem).wait()
 
     def cols(h):
         return pl.ds(h * half, half)
 
-    copies, inner_copies = {}, {}
+    copies = {}
     for name, src, buf in (("r", rt, rb), ("g", gt, gb)):
         for d in range(chips):
             if d:
@@ -179,6 +194,8 @@
                 copies[(name,) + lead + (d, h)] = remote(
                     (name,) + lead + (d, h), first.at[:, cols(h)], buf.at[2 * d, :, cols(h)], across[d]
                 )
+            if lead == (1,) and (3, h) in ALONG:
+                continue
             via, to = (1, 2) if h == 0 else (2, 1)
             copies[(name,) + lead + (3, h)] = remote(
                 (name,) + lead + (3, h), buf.at[2 * via, :, cols(h)], buf.at[6, :, cols(h)], across[to]
@@ -187,7 +204,7 @@
     spread("x", tok, xb, ())
     for d in range(chips):
         for h in range(HALVES):
-            for key, first, buf in ((("xc",), tok, xb), (("dc", 0), dy, every.at[0])):
+            for key, first, buf in ((("xc",), tok, xb), (("dc",), dy, every.at[0])):
                 copies[key + (d, h)] = remote(
                     key + (d, h),
                     buf.at[2 * d, :, cols(h)] if d else first.at[:, cols(h)],
@@ -198,8 +215,8 @@
         spread("d", every.at[k, 0] if k else dy, every.at[k], (k,))
         if k:
             for d in range(chips):
-                copies["dc", k, d] = remote(
-                    ("dc", k, d), every.at[k, 2 * d], every.at[k, 2 * d + 1], partner
+                copies["dk", k, d] = remote(
+                    ("dk", k, d), every.at[k, 2 * d], every.at[k, 2 * d + 1], partner
                 )
             copies["z", k] = remote(("z", k), dy, every.at[k, 0], above[k])
     for d, h in ALONG:
@@ -222,31 +239,42 @@
     def start(*key):
         copies[key].start()
 
-    def arrive(*key):
-        copies[key].wait_recv()
-
-    def relay(name, lead=()):
+    def arrive(group, ref):
+        whole(ref, rsem.at[groups[group]])
+
+    def place(lead):
+        return xb if lead == ("x",) else every.at[lead[1]]
+
+    def relay(*lead):
         for d, h in ((1, 0), (2, 1)):
-            arrive(name, *lead, d, h)
-            if name == "x" or lead[0] != 1 or (3, h) not in ALONG:
-                start(name, *lead, 3, h)
-            if name == "x" or lead[0] == 0:
-                start(name + "c", *lead, d, h)
-
-    def rest(name, lead=()):
+            arrive(lead + (d, h), place(lead).at[2 * d, :, cols(h)])
+            if lead != ("d", 1) or (3, h) not in ALONG:
+                start(*lead, 3, h)
+            if lead in (("x",), ("d", 0)):
+                start(lead[0] + "c", d, h)
+
+    def rest(*lead):
+        arrive(lead + ("rest",), place(lead).at[2])
         for d, h in ((1, 1), (2, 0)):
-            arrive(name, *lead, d, h)
-            if name == "x" or lead[0] == 0:
-                start(name + "c", *lead, d, h)
+            if lead in (("x",), ("d", 0)):
+                start(lead[0] + "c", d, h)
             else:
-                start("dc", *lead, d)
-
-    def send_plane(k):
+                start("dk", lead[1], d)
+
+    def diagonal_in(*lead):
+        arrive(lead + (3,), place(lead).at[6])
+        if lead in (("x",), ("d", 0)):
+            for h in range(HALVES):
+                start(lead[0] + "c", 3, h)
+        else:
+            start("dk", lead[1], 3)
+
+    def plane_in(k):
+        arrive(("z", k), every.at[k, 0])
         for h in range(HALVES):
             for d in (1, 2):
-                piece = (d, h if d == 1 else 1 - h)
-                if k != 1 or piece not in ALONG:
-                    start("d", k, *piece)
+                start("d", k, d, h if d == 1 else 1 - h)
+        start("dk", k, 0)
 
     barrier = pltpu.get_barrier_semaphore()
     for target in [partner] + across[1:3] + [above[1]]:
@@ -263,18 +291,21 @@
         pl.semaphore_signal(known, inc=1, device_id=above[3], device_id_type=MESH)
         copies["z", 3].start()
 
-    send_plane(0)
+    for h in range(HALVES):
+        for d in (1, 2):
+            start("d", 0, d, h if d == 1 else 1 - h)
     start("z", 1)
     for h in range(HALVES):
-        start("dc", 0, 0, h)
+        start("dc", 0, h)
     for name in ("r", "g"):
         for d in (1, 2):
             start(name, d)
         start(name + "c", 0)
     for h in range(HALVES):
-        start("x", 1, h)
-        start("x", 2, 1 - h)
+        for d in (1, 2):
+            start("x", d, h if d == 1 else 1 - h)
         start("xc", 0, h)
+    load_weights()
 
     @pl.when(inner)
     def _():
@@ -282,8 +313,8 @@
         pl.semaphore_signal(known, inc=1, device_id=above[1], device_id_type=MESH)
         copies["z", 2].start()
 
-    relay("d", (0,))
-    rest("d", (0,))
+    relay("d", 0)
+    rest("d", 0)
     for name in ("r", "g"):
         start(name, 3)
 
@@ -295,48 +326,34 @@
 
     relay("x")
     rest("x")
-    for name in ("r", "g"):
-        for d in (1, 2):
-            arrive(name, d)
-            start(name + "c", d)
-    arrive("z", 1)
-    send_plane(1)
-    start("dc", 1, 0)
-    for h in range(HALVES):
-        arrive("d", 0, 3, h)
-        start("dc", 0, 3, h)
+    for c in own:
+        c.wait()
+    plane_in(1)
+    diagonal_in("d", 0)
     for d, h in ALONG:
         start("d", 1, d, h)
+    plane_in(2)
+    diagonal_in("x")
+    for name, buf in (("r", rb), ("g", gb)):
+        arrive(name, buf.at[pl.ds(0, chips - 1)])
+        for d in range(1, chips):
+            start(name + "c", d)
+    plane_in(3)
+
+    whole(wdv, lsem.at[4])
     for h in range(HALVES):
-        arrive("x", 3, h)
-        start("xc", 3, h)
-    for name in ("r", "g"):
-        arrive(name, 3)
-        start(name + "c", 3)
-
-    for c in own:
-        c.wait()
-    for c in down_loads:
-        c.wait()
-    for h in range(HALVES):
-        for d in range(chips):
-            arrive("dc", 0, d, h)
+        arrive(("dc", h), every.at[0, pl.ds(0, chips), :, cols(h)])
         begin = h * half
         term = lax.dot_general(
-            wdv[:, begin : begin + half],
+            wdv[:, :, begin : begin + half].reshape(local_experts * hidden_units, half),
             every[0, :, :, begin : begin + half].reshape(count, half),
             NT,
             preferred_element_type=jnp.float32,
         ).T
         grads[...] = grads[...] + term if h else term
-    arrive("z", 2)
-    send_plane(2)
-    start("dc", 2, 0)
-    for c in gate_up_loads:
-        c.wait()
+    whole(wide, lsem.at[5])
     for h in range(HALVES):
-        for d in range(chips):
-            arrive("xc", d, h)
+        arrive(("xc", h), xb.at[pl.ds(0, chips), :, cols(h)])
         begin = h * half
         term = jnp.dot(
             xb[:, :, begin : begin + half].reshape(count, half),
@@ -345,13 +362,10 @@
         )
         pre[...] = pre[...] + term if h else term
         if h == 0:
-            relay("d", (1,))
-    arrive("z", 3)
-    send_plane(3)
-    start("dc", 3, 0)
-    for name in ("r", "g"):
-        for d in range(chips):
-            arrive(name + "c", d)
+            relay("d", 1)
+    rest("d", 1)
+    arrive("rc", rb.at[pl.ds(0, chips)])
+    arrive("gc", gb.at[pl.ds(0, chips)])
 
     named, given = rb[...], gb[...]
     diagonal = lax.broadcasted_iota(jnp.int32, (1, rows, rows), 1) == lax.broadcasted_iota(
@@ -371,7 +385,6 @@
         both[:, a:b] = (hidden_grad * up_pre * (s + gate_pre * s * (1.0 - s))).astype(jnp.bfloat16)
         both[:, b:c] = (hidden_grad * silu).astype(jnp.bfloat16)
 
-    hid_loads = []
     for j in range(PARTS + 1):
         if j < PARTS:
             total = lax.dot_general(
@@ -381,7 +394,7 @@
             start("p", j)
             keep[j] = total[:, 0]
         if j == 0:
-            rest("d", (1,))
+            relay("d", 2)
         if j == 1:
             for e in range(local_experts):
                 hid_out[e] = hid_f[e].T.astype(jnp.bfloat16)
@@ -390,15 +403,16 @@
                     start("h", k, e)
             first = pl.multiple_of(plane * share, 16)
             for e in range(local_experts):
-                hid_loads.append(load(hid_out.at[e, pl.ds(first, share)], hid_in.at[0, e]))
-            relay("d", (2,))
+                load(hid_out.at[e, pl.ds(first, share)], hid_in.at[0, e], 6)
+            relay("d", 3)
         if j == 2:
-            rest("d", (2,))
+            rest("d", 2)
+            diagonal_in("d", 1)
         if j == 3:
-            relay("d", (3,))
+            rest("d", 3)
         if j:
             i = j - 1
-            arrive("p", i)
+            arrive(("p", i), pair_in.at[i])
             total = keep[i] + pair_in[i].astype(jnp.float32)
             for d in range(chips - 1, 0, -1):
                 ret_out[i, d] = total[d].astype(jnp.bfloat16)
@@ -406,23 +420,19 @@
                 start("t", i, d)
             own_sum[:, i * width : (i + 1) * width] = total[0]
 
-    rest("d", (3,))
+    diagonal_in("d", 2)
+    diagonal_in("d", 3)
+    arrive("h", hid_in.at[pl.ds(1, planes - 1)])
     for k in range(1, planes):
-        for h in range(HALVES):
-            arrive("d", k, 3, h)
-        start("dc", k, 3)
-    for k in range(1, planes):
-        for e in range(local_experts):
-            arrive("h", k, e)
-        for d in range(chips):
-            arrive("dc", k, d)
-    for j in range(PARTS):
-        for d in range(1, chips):
-            arrive("t", j, d)
-    for c in hid_loads:
-        c.wait()
-    for c in copies.values():
-        c.wait_send()
+        arrive(("dk", k), every.at[k, pl.ds(0, chips)])
+    arrive("t", ret_in)
+    whole(hid_in.at[0], lsem.at[6])
+    sent = sum(
+        math.prod(c.src_ref.shape) for key, c in copies.items() if key[0][0] not in ("r", "g")
+    )
+    whole(wide.at[pl.ds(0, sent // wide.shape[1])], ssem.at[0])
+    for i, buf in ((1, rb), (2, gb)):
+        whole(buf.at[pl.ds(0, 2 * chips - 1)], ssem.at[i])
 
 
 def finish_kernel(
@@ -474,7 +484,7 @@
         ((2 * chips, top, rows), jnp.int32),
         ((2 * chips, top, rows), f32),
         ((model_width, 2 * local_experts * hidden_units), bf16),
-        ((local_experts * hidden_units, model_width), bf16),
+        ((local_experts, hidden_units, model_width), bf16),
         ((count, 2 * local_experts * hidden_units), f32),
         ((count, local_experts * hidden_units), f32),
         ((local_experts, count, hidden_units), f32),
@@ -523,7 +533,7 @@
     rows, model_width = tokens.shape
     local_experts, _, hidden_units = w_gate.shape
     share = hidden_units // planes
-    amount = len(copy_keys(chips, planes, local_experts))
+    amount = len(arrival_groups(planes))
     count = 2 * chips * rows
     outside = pl.BlockSpec(memory_space=pltpu.HBM)
     inside = pl.BlockSpec(memory_space=pltpu.VMEM)
@@ -539,8 +549,8 @@
         out_specs=(inside,) * 4,
         scratch_shapes=[pltpu.VMEM(dims, kind) for dims, kind in shapes]
         + [
-            pltpu.SemaphoreType.DMA((4 + 5 * local_experts,)),
-            pltpu.SemaphoreType.DMA((amount,)),
+            pltpu.SemaphoreType.DMA((7,)),
+            pltpu.SemaphoreType.DMA((3,)),
             pltpu.SemaphoreType.DMA((amount,)),
             pltpu.SemaphoreType.REGULAR,
         ],

time: 29 us -> 28.5 us (0.983)
  Pallas kernels: 28.2 us -> 27.7 us
    pallas_call x1, Pallas kernels: 26.5 us -> 26 us  [shards(): pl.pallas_call(functools.partial(fused_kernel, chips, planes), out_shape=...]
where the time goes in v2:
time: 28.5 us; the launch traced here: 28.4 us
  Pallas kernels  27.7 us (97%)
  between operations  0.64 us (2%)
    pallas_call x1, Pallas kernels, shards(): pl.pallas_call(functools.partial(fused_kernel, chips, planes), out_shape=...  26 us
    pallas_call x1, Pallas kernels, shards(): pl.pallas_call(finish_kernel, out_shape=(jax.ShapeDtypeStruct((rows, mode...  1.75 us

profile of v2, /device:TPU:0, one launch (start us, length us, event | category | flops | bytes accessed | tf_op | source)
XLA Modules:
  0.0 28.4 jit_solution(7212132308312648655)
XLA Ops:
  0.6 26.0 %expert_backward.1 = (bf16[4,8,16,2048]{3,2,1,0:T(8,128)(2,1)S(1)}, bf16[4,2,96,128]{3,2,1,0:T(8,128)(2,1)S(1)}, f32[16,2048]{1,0:T(8,128)S(1)}, bf16[3,16,2048]{2,1,0:T(8,128)(2,1)S(1)}) custom-call(bf16[16,2048]{1,0:T(8,128)(2,1)} %tok.1, bf16[16,2048]{1,0:T(8,128)(2,1)} %dy.1, s32[8,16]{1,0:T(8,128)} %bitcast.7, f32[8,16]{1,0:T(8,128)} %bitcast.8, ...), custom_call_target="tpu_custom_call" | custom-call | tf_op jit(solution)/shard_map/expert_backward/pallas_call | solution.py:540
  26.6 1.7 %expert_finish.1 = (bf16[16,2048]{1,0:T(8,128)(2,1)}, f32[96,32,128]{2,1,0:T(8,128)}) custom-call(bf16[4,8,16,2048]{3,2,1,0:T(8,128)(2,1)S(1)} %get-tuple-element.8.every, bf16[4,2,96,128]{3,2,1,0:T(8,128)(2,1)S(1)} %get-tuple-element.9.hid, f32[16,2048]{1,0:T(8,128)S(1)} %get-tuple-element.10.own_sum, bf16[3,16,2048]{2,1,0:T(8,128)(2,1)S(1)} %get-tuple-element.11.returned), custom_call_target="tpu_custom_call" | custom-call | tf_op jit(solution)/shard_map/expert_finish/pallas_call | solution.py:564

commit v3 on v2

--- a/solution.py
+++ b/solution.py
@@ -131,8 +131,8 @@
 
 
 def fused_kernel(
-    chips, planes, tok, dy, rt, gt, wg, wu, wd, every, hid_in, own_sum, ret_in,
-    xb, rb, gb, wide, wdv, pre, grads, hid_f, hid_out, both,
+    chips, planes, tok, dy, rt, gt, wg, wu, wd, down_v, own_sum, ret_in,
+    every, hid_in, xb, rb, gb, wide, wdv, pre, grads, hid_out, both,
     keep, pair_out, pair_in, ret_out, lsem, ssem, rsem, known,
 ):
     local_experts, model_width, hidden_units = wg.shape
@@ -313,45 +313,45 @@
         pl.semaphore_signal(known, inc=1, device_id=above[1], device_id_type=MESH)
         copies["z", 2].start()
 
-    relay("d", 0)
-    rest("d", 0)
-    for name in ("r", "g"):
-        start(name, 3)
-
     @pl.when(jnp.logical_not(inner))
     def _():
         pl.semaphore_wait(known, 1)
         copies["z", 3].start()
         copies["z", 2].start()
 
+    relay("d", 0)
+    rest("d", 0)
+    for name in ("r", "g"):
+        start(name, 3)
+
     relay("x")
     rest("x")
     for c in own:
         c.wait()
-    plane_in(1)
     diagonal_in("d", 0)
     for d, h in ALONG:
         start("d", 1, d, h)
-    plane_in(2)
+    plane_in(1)
     diagonal_in("x")
     for name, buf in (("r", rb), ("g", gb)):
         arrive(name, buf.at[pl.ds(0, chips - 1)])
         for d in range(1, chips):
             start(name + "c", d)
-    plane_in(3)
+    plane_in(2)
 
     whole(wdv, lsem.at[4])
     for h in range(HALVES):
         arrive(("dc", h), every.at[0, pl.ds(0, chips), :, cols(h)])
         begin = h * half
         term = lax.dot_general(
+            every[0, :, :, begin : begin + half].reshape(count, half),
             wdv[:, :, begin : begin + half].reshape(local_experts * hidden_units, half),
-            every[0, :, :, begin : begin + half].reshape(count, half),
             NT,
             preferred_element_type=jnp.float32,
-        ).T
+        )
         grads[...] = grads[...] + term if h else term
     whole(wide, lsem.at[5])
+    plane_in(3)
     for h in range(HALVES):
         arrive(("xc", h), xb.at[pl.ds(0, chips), :, cols(h)])
         begin = h * half
@@ -361,8 +361,7 @@
             preferred_element_type=jnp.float32,
         )
         pre[...] = pre[...] + term if h else term
-        if h == 0:
-            relay("d", 1)
+    relay("d", 1)
     rest("d", 1)
     arrive("rc", rb.at[pl.ds(0, chips)])
     arrive("gc", gb.at[pl.ds(0, chips)])
@@ -381,33 +380,30 @@
         gate_pre, up_pre = pre[:, a:b], pre[:, b:c]
         s = jax.nn.sigmoid(gate_pre)
         silu = gate_pre * s
-        hid_f[e] = silu * up_pre * gain
+        hid_out[e] = (silu * up_pre * gain).T.astype(jnp.bfloat16)
         both[:, a:b] = (hidden_grad * up_pre * (s + gate_pre * s * (1.0 - s))).astype(jnp.bfloat16)
         both[:, b:c] = (hidden_grad * silu).astype(jnp.bfloat16)
+
+    for k in range(planes - 1, 0, -1):
+        for e in range(local_experts):
+            start("h", k, e)
+    first = pl.multiple_of(plane * share, 16)
+    for e in range(local_experts):
+        load(hid_out.at[e, pl.ds(first, share)], hid_in.at[0, e], 6)
 
     for j in range(PARTS + 1):
         if j < PARTS:
             total = lax.dot_general(
-                wide[j * width : (j + 1) * width, :], both[...], NT, preferred_element_type=jnp.float32
-            ).T.reshape(chips, 2, rows, width)
+                both[...], wide[j * width : (j + 1) * width, :], NT, preferred_element_type=jnp.float32
+            ).reshape(chips, 2, rows, width)
             pair_out[j] = total[:, 1].astype(jnp.bfloat16)
             start("p", j)
             keep[j] = total[:, 0]
         if j == 0:
             relay("d", 2)
-        if j == 1:
-            for e in range(local_experts):
-                hid_out[e] = hid_f[e].T.astype(jnp.bfloat16)
-            for k in range(1, planes):
-                for e in range(local_experts):
-                    start("h", k, e)
-            first = pl.multiple_of(plane * share, 16)
-            for e in range(local_experts):
-                load(hid_out.at[e, pl.ds(first, share)], hid_in.at[0, e], 6)
+        if j == 2:
             relay("d", 3)
-        if j == 2:
             rest("d", 2)
-            diagonal_in("d", 1)
         if j == 3:
             rest("d", 3)
         if j:
@@ -420,41 +416,20 @@
                 start("t", i, d)
             own_sum[:, i * width : (i + 1) * width] = total[0]
 
-    diagonal_in("d", 2)
-    diagonal_in("d", 3)
+    for k in range(1, planes):
+        diagonal_in("d", k)
+    whole(hid_in.at[0], lsem.at[6])
     arrive("h", hid_in.at[pl.ds(1, planes - 1)])
+    pieces = [hid_in[k].reshape(local_experts * share, count) for k in range(planes)]
+    pieces = jnp.concatenate(pieces, axis=1)
     for k in range(1, planes):
         arrive(("dk", k), every.at[k, pl.ds(0, chips)])
-    arrive("t", ret_in)
-    whole(hid_in.at[0], lsem.at[6])
-    sent = sum(
-        math.prod(c.src_ref.shape) for key, c in copies.items() if key[0][0] not in ("r", "g")
-    )
-    whole(wide.at[pl.ds(0, sent // wide.shape[1])], ssem.at[0])
-    for i, buf in ((1, rb), (2, gb)):
-        whole(buf.at[pl.ds(0, 2 * chips - 1)], ssem.at[i])
-
-
-def finish_kernel(
-    every, hid, own_sum, returned, token_out, down_out, token_v, down_v, sems
-):
-    planes, local_experts, share, count = hid.shape
-    model_width = every.shape[3]
-    width = model_width // STEPS
-    blocks = width // 128
-    stores = []
-
-    def store(src, dst):
-        c = pltpu.make_async_copy(src, dst, sems.at[len(stores)])
-        c.start()
-        stores.append(c)
-
-    pieces = [hid[k].reshape(local_experts * share, count) for k in range(planes)]
-    pieces = jnp.concatenate(pieces, axis=1)
+    step = model_width // STEPS
+    blocks = step // 128
     for i in range(STEPS):
         result = jnp.dot(
             pieces,
-            every[:, :, :, i * width : (i + 1) * width].reshape(planes * count, width),
+            every[:, :, :, i * step : (i + 1) * step].reshape(planes * count, step),
             preferred_element_type=jnp.float32,
         )
         lines = down_v.at[i].reshape(share * blocks * local_experts, 128)
@@ -463,15 +438,31 @@
                 lines[pl.ds(b * local_experts + e, share, stride=blocks * local_experts), :] = (
                     result[e * share : (e + 1) * share, b * 128 : (b + 1) * 128]
                 )
-        store(
-            down_v.at[i], down_out.at[:, pl.ds(i * blocks * local_experts, blocks * local_experts)]
-        )
-        if i == 0:
-            total = own_sum[...]
-            for d in range(returned.shape[0]):
-                total = total + returned[d].astype(jnp.float32)
-            token_v[...] = total.astype(jnp.bfloat16)
-            store(token_v, token_out)
+    arrive("t", ret_in)
+    sent = sum(
+        math.prod(c.src_ref.shape) for key, c in copies.items() if key[0][0] not in ("r", "g")
+    )
+    whole(wide.at[pl.ds(0, sent // wide.shape[1])], ssem.at[0])
+    for i, buf in ((1, rb), (2, gb)):
+        whole(buf.at[pl.ds(0, 2 * chips - 1)], ssem.at[i])
+
+
+def finish_kernel(down_v, own_sum, returned, token_out, down_out, token_v, sems):
+    stores = []
+
+    def store(src, dst):
+        c = pltpu.make_async_copy(src, dst, sems.at[len(stores)])
+        c.start()
+        stores.append(c)
+
+    lines = down_v.shape[2]
+    for i in range(down_v.shape[0]):
+        store(down_v.at[i], down_out.at[:, pl.ds(i * lines, lines)])
+    total = own_sum[...]
+    for d in range(returned.shape[0]):
+        total = total + returned[d].astype(jnp.float32)
+    token_v[...] = total.astype(jnp.bfloat16)
+    store(token_v, token_out)
     for c in stores:
         c.wait()
 
@@ -479,7 +470,10 @@
 def fused_shapes(chips, planes, rows, top, local_experts, model_width, hidden_units):
     bf16, f32 = jnp.bfloat16, jnp.float32
     count, width = 2 * chips * rows, model_width // PARTS
+    share = hidden_units // planes
     return [
+        ((planes, 2 * chips, rows, model_width), bf16),
+        ((planes, local_experts, share, count), bf16),
         ((2 * chips, rows, model_width), bf16),
         ((2 * chips, top, rows), jnp.int32),
         ((2 * chips, top, rows), f32),
@@ -487,7 +481,6 @@
         ((local_experts, hidden_units, model_width), bf16),
         ((count, 2 * local_experts * hidden_units), f32),
         ((count, local_experts * hidden_units), f32),
-        ((local_experts, count, hidden_units), f32),
         ((local_experts, hidden_units, count), bf16),
         ((count, 2 * local_experts * hidden_units), bf16),
         ((PARTS, chips, rows, width), f32),
@@ -519,7 +512,7 @@
     shapes = fused_shapes(
         chips, planes, rows, routes.shape[1], local_experts, model_width, hidden_units
     )
-    passed = planes * groups * rows * model_width * 2
+    passed = 4 * hidden_units // planes * local_experts * model_width
     if buffer_bytes(shapes) > VMEM_BUDGET or passed > VMEM_PASSED:
         return None
     return chips, planes, shapes
@@ -534,19 +527,18 @@
     local_experts, _, hidden_units = w_gate.shape
     share = hidden_units // planes
     amount = len(arrival_groups(planes))
-    count = 2 * chips * rows
+    lines = model_width // STEPS // 128 * local_experts
     outside = pl.BlockSpec(memory_space=pltpu.HBM)
     inside = pl.BlockSpec(memory_space=pltpu.VMEM)
     passed = pl.pallas_call(
         functools.partial(fused_kernel, chips, planes),
         out_shape=(
-            pltpu.VMEM((planes, 2 * chips, rows, model_width), jnp.bfloat16),
-            pltpu.VMEM((planes, local_experts, share, count), jnp.bfloat16),
+            pltpu.VMEM((STEPS, share, lines, 128), jnp.float32),
             pltpu.VMEM((rows, model_width), jnp.float32),
             pltpu.VMEM((chips - 1, rows, model_width), jnp.bfloat16),
         ),
         in_specs=[outside] * 7,
-        out_specs=(inside,) * 4,
+        out_specs=(inside,) * 3,
         scratch_shapes=[pltpu.VMEM(dims, kind) for dims, kind in shapes]
         + [
             pltpu.SemaphoreType.DMA((7,)),
@@ -559,19 +551,16 @@
         ),
         name="expert_backward",
     )(tokens, out_grad, routes.T, route_gates.T, w_gate, w_up, w_down)
-    width = model_width // STEPS
-    lines = width // 128 * local_experts
     token_grad, down_grad = pl.pallas_call(
         finish_kernel,
         out_shape=(
             jax.ShapeDtypeStruct((rows, model_width), jnp.bfloat16),
             jax.ShapeDtypeStruct((share, model_width // 128 * local_experts, 128), jnp.float32),
         ),
-        in_specs=[inside] * 4,
+        in_specs=[inside] * 3,
         out_specs=(outside,) * 2,
         scratch_shapes=[
             pltpu.VMEM((rows, model_width), jnp.bfloat16),
-            pltpu.VMEM((STEPS, share, lines, 128), jnp.float32),
             pltpu.SemaphoreType.DMA((1 + STEPS,)),
         ],
         compiler_params=pltpu.CompilerParams(vmem_limit_bytes=32 << 20),

time: 28.5 us -> 26.6 us (0.933)
  Pallas kernels: 27.7 us -> 25.8 us
    pallas_call x1, Pallas kernels: 26 us -> 24.6 us  [shards(): pl.pallas_call(functools.partial(fused_kernel, chips, planes), out_shape=...]
    pallas_call x1, Pallas kernels: 1.75 us -> 1.18 us  [shards(): pl.pallas_call(finish_kernel, out_shape=(jax.ShapeDtypeStruct((rows, mode...]
where the time goes in v3:
time: 26.6 us; the launch traced here: 26.4 us
  Pallas kernels  25.8 us (97%)
  between operations  0.64 us (2%)
    pallas_call x1, Pallas kernels, shards(): pl.pallas_call(functools.partial(fused_kernel, chips, planes), out_shape=...  24.6 us
    pallas_call x1, Pallas kernels, shards(): pl.pallas_call(finish_kernel, out_shape=(jax.ShapeDtypeStruct((rows, mode...  1.18 us

profile of v3, /device:TPU:0, one launch (start us, length us, event | category | flops | bytes accessed | tf_op | source)
XLA Modules:
  0.0 26.4 jit_solution(17696374158236472484)
XLA Ops:
  0.6 24.6 %expert_backward.1 = (f32[2,96,16,128]{3,2,1,0:T(8,128)S(1)}, f32[16,2048]{1,0:T(8,128)S(1)}, bf16[3,16,2048]{2,1,0:T(8,128)(2,1)S(1)}) custom-call(bf16[16,2048]{1,0:T(8,128)(2,1)} %tok.1, bf16[16,2048]{1,0:T(8,128)(2,1)} %dy.1, s32[8,16]{1,0:T(8,128)} %bitcast.7, f32[8,16]{1,0:T(8,128)} %bitcast.8, bf16[2,2048,384]{2,1,0:T(8,128)(2,1)} %wg.1, ...), custom_call_target="tpu_custom_call" | custom-call | tf_op jit(solution)/shard_map/expert_backward/pallas_call | solution.py:533
  25.2 1.2 %expert_finish.1 = (bf16[16,2048]{1,0:T(8,128)(2,1)}, f32[96,32,128]{2,1,0:T(8,128)}) custom-call(f32[2,96,16,128]{3,2,1,0:T(8,128)S(1)} %get-tuple-element.7.down_v, f32[16,2048]{1,0:T(8,128)S(1)} %get-tuple-element.8.own_sum, bf16[3,16,2048]{2,1,0:T(8,128)(2,1)S(1)} %get-tuple-element.9.returned), custom_call_target="tpu_custom_call" | custom-call | tf_op jit(solution)/shard_map/expert_finish/pallas_call | solution.py:554

commit v4 on v3

--- a/solution.py
+++ b/solution.py
@@ -104,11 +104,10 @@
 
 
 def arrival_groups(planes):
-    names = ["r", "g", "rc", "gc", "h", "t"]
+    names = ["r", "g", "rc", "gc", "h", "t", "first", "xc", "dc"]
     names += [("z", k) for k in range(1, planes)]
     for lead in [("x",)] + [("d", k) for k in range(planes)]:
         names += [lead + (1, 0), lead + (2, 1), lead + ("rest",), lead + (3,)]
-    names += [(name, h) for name in ("xc", "dc") for h in range(HALVES)]
     names += [("dk", k) for k in range(1, planes)] + [("p", j) for j in range(PARTS)]
     return {name: i for i, name in enumerate(names)}
 
@@ -120,7 +119,7 @@
     if name in ("r", "g", "rc", "gc", "h", "t"):
         return name
     if name in ("xc", "dc"):
-        return (name, key[2])
+        return "first" if key[:2] == ("xc", 0) else name
     if name == "dk":
         return key[:2]
     d, h = key[-2:]
@@ -291,21 +290,22 @@
         pl.semaphore_signal(known, inc=1, device_id=above[3], device_id_type=MESH)
         copies["z", 3].start()
 
-    for h in range(HALVES):
-        for d in (1, 2):
-            start("d", 0, d, h if d == 1 else 1 - h)
+    def send_own(*lead):
+        for h in range(HALVES):
+            for d in (1, 2):
+                start(*lead, d, h if d == 1 else 1 - h)
+        for h in range(HALVES):
+            start(lead[0] + "c", 0, h)
+
+    send_own("x")
     start("z", 1)
-    for h in range(HALVES):
-        start("dc", 0, h)
     for name in ("r", "g"):
         for d in (1, 2):
             start(name, d)
         start(name + "c", 0)
-    for h in range(HALVES):
-        for d in (1, 2):
-            start("x", d, h if d == 1 else 1 - h)
-        start("xc", 0, h)
     load_weights()
+    arrive("first", xb.at[1])
+    send_own("d", 0)
 
     @pl.when(inner)
     def _():
@@ -313,56 +313,37 @@
         pl.semaphore_signal(known, inc=1, device_id=above[1], device_id_type=MESH)
         copies["z", 2].start()
 
+    relay("x")
+    for name in ("r", "g"):
+        start(name, 3)
+
     @pl.when(jnp.logical_not(inner))
     def _():
         pl.semaphore_wait(known, 1)
         copies["z", 3].start()
         copies["z", 2].start()
 
+    rest("x")
     relay("d", 0)
     rest("d", 0)
-    for name in ("r", "g"):
-        start(name, 3)
-
-    relay("x")
-    rest("x")
     for c in own:
         c.wait()
-    diagonal_in("d", 0)
-    for d, h in ALONG:
-        start("d", 1, d, h)
-    plane_in(1)
     diagonal_in("x")
     for name, buf in (("r", rb), ("g", gb)):
         arrive(name, buf.at[pl.ds(0, chips - 1)])
         for d in range(1, chips):
             start(name + "c", d)
+    diagonal_in("d", 0)
+    for d, h in ALONG:
+        start("d", 1, d, h)
+    plane_in(1)
+
+    whole(wide, lsem.at[5])
+    arrive("xc", xb.at[pl.ds(0, chips - 1)])
+    pre[...] = jnp.dot(
+        xb[...].reshape(count, model_width), wide[...], preferred_element_type=jnp.float32
+    )
     plane_in(2)
-
-    whole(wdv, lsem.at[4])
-    for h in range(HALVES):
-        arrive(("dc", h), every.at[0, pl.ds(0, chips), :, cols(h)])
-        begin = h * half
-        term = lax.dot_general(
-            every[0, :, :, begin : begin + half].reshape(count, half),
-            wdv[:, :, begin : begin + half].reshape(local_experts * hidden_units, half),
-            NT,
-            preferred_element_type=jnp.float32,
-        )
-        grads[...] = grads[...] + term if h else term
-    whole(wide, lsem.at[5])
-    plane_in(3)
-    for h in range(HALVES):
-        arrive(("xc", h), xb.at[pl.ds(0, chips), :, cols(h)])
-        begin = h * half
-        term = jnp.dot(
-            xb[:, :, begin : begin + half].reshape(count, half),
-            wide[begin : begin + half, :],
-            preferred_element_type=jnp.float32,
-        )
-        pre[...] = pre[...] + term if h else term
-    relay("d", 1)
-    rest("d", 1)
     arrive("rc", rb.at[pl.ds(0, chips)])
     arrive("gc", gb.at[pl.ds(0, chips)])
 
@@ -376,20 +357,35 @@
         )
         gain = jnp.sum(jnp.where(diagonal, gain, 0.0), axis=2, keepdims=True).reshape(count, 1)
         a, b, c = ((2 * e + i) * hidden_units for i in range(3))
-        hidden_grad = gain * grads[:, e * hidden_units : (e + 1) * hidden_units]
         gate_pre, up_pre = pre[:, a:b], pre[:, b:c]
         s = jax.nn.sigmoid(gate_pre)
-        silu = gate_pre * s
-        hid_out[e] = (silu * up_pre * gain).T.astype(jnp.bfloat16)
-        both[:, a:b] = (hidden_grad * up_pre * (s + gate_pre * s * (1.0 - s))).astype(jnp.bfloat16)
-        both[:, b:c] = (hidden_grad * silu).astype(jnp.bfloat16)
-
+        silu = gate_pre * s * gain
+        hid_out[e] = (silu * up_pre).T.astype(jnp.bfloat16)
+        pre[:, a:b] = up_pre * (s + gate_pre * s * (1.0 - s)) * gain
+        pre[:, b:c] = silu
     for k in range(planes - 1, 0, -1):
         for e in range(local_experts):
             start("h", k, e)
     first = pl.multiple_of(plane * share, 16)
     for e in range(local_experts):
         load(hid_out.at[e, pl.ds(first, share)], hid_in.at[0, e], 6)
+
+    whole(wdv, lsem.at[4])
+    arrive("dc", every.at[0, pl.ds(0, chips)])
+    grads[...] = lax.dot_general(
+        every[0].reshape(count, model_width),
+        wdv[...].reshape(local_experts * hidden_units, model_width),
+        NT,
+        preferred_element_type=jnp.float32,
+    )
+    plane_in(3)
+    relay("d", 1)
+    rest("d", 1)
+    for e in range(local_experts):
+        hidden_grad = grads[:, e * hidden_units : (e + 1) * hidden_units]
+        for i in (2 * e, 2 * e + 1):
+            part = slice(i * hidden_units, (i + 1) * hidden_units)
+            both[:, part] = (hidden_grad * pre[:, part]).astype(jnp.bfloat16)
 
     for j in range(PARTS + 1):
         if j < PARTS:

time: 26.6 us -> 24.9 us (0.936)
  Pallas kernels: 25.8 us -> 24.1 us
    pallas_call x1, Pallas kernels: 24.6 us -> 22.9 us  [shards(): pl.pallas_call(functools.partial(fused_kernel, chips, planes), out_shape=...]
where the time goes in v4:
time: 24.9 us; the launch traced here: 24.7 us
  Pallas kernels  24.1 us (97%)
  between operations  0.64 us (3%)
    pallas_call x1, Pallas kernels, shards(): pl.pallas_call(functools.partial(fused_kernel, chips, planes), out_shape=...  22.9 us
    pallas_call x1, Pallas kernels, shards(): pl.pallas_call(finish_kernel, out_shape=(jax.ShapeDtypeStruct((rows, mode...  1.18 us

profile of v4, /device:TPU:0, one launch (start us, length us, event | category | flops | bytes accessed | tf_op | source)
XLA Modules:
  0.0 24.7 jit_solution(7222833682929725356)
XLA Ops:
  0.6 22.9 %expert_backward.1 = (f32[2,96,16,128]{3,2,1,0:T(8,128)S(1)}, f32[16,2048]{1,0:T(8,128)S(1)}, bf16[3,16,2048]{2,1,0:T(8,128)(2,1)S(1)}) custom-call(bf16[16,2048]{1,0:T(8,128)(2,1)} %tok.1, bf16[16,2048]{1,0:T(8,128)(2,1)} %dy.1, s32[8,16]{1,0:T(8,128)} %bitcast.7, f32[8,16]{1,0:T(8,128)} %bitcast.8, bf16[2,2048,384]{2,1,0:T(8,128)(2,1)} %wg.1, ...), custom_call_target="tpu_custom_call" | custom-call | tf_op jit(solution)/shard_map/expert_backward/pallas_call | solution.py:529
  23.5 1.2 %expert_finish.1 = (bf16[16,2048]{1,0:T(8,128)(2,1)}, f32[96,32,128]{2,1,0:T(8,128)}) custom-call(f32[2,96,16,128]{3,2,1,0:T(8,128)S(1)} %get-tuple-element.7.down_v, f32[16,2048]{1,0:T(8,128)S(1)} %get-tuple-element.8.own_sum, bf16[3,16,2048]{2,1,0:T(8,128)(2,1)S(1)} %get-tuple-element.9.returned), custom_call_target="tpu_custom_call" | custom-call | tf_op jit(solution)/shard_map/expert_finish/pallas_call | solution.py:550
